TPU v7x, 512 devices: a whole 4x4x16 slice. The times are simulated.
512 devices in a mesh: space: 64 (over z_lo, x, core), tm: 8 (over y, z_hi).
Axes of the slice: x: 4, y: 4, z: 16 (z_hi: 2, z_lo: 8; z = z_hi * 8 + z_lo), core: 2. Of those that a mesh axis runs over, the one named last changes fastest.
Arguments:
- query_key: bfloat16 [1, 65536, 64], P(None, 'space'), may hold values from -1.5 to 8
- selection: bfloat16 [1, 65536, 64], P(None, 'space'), may hold values from 0.19921875 to 1
- memory_key: bfloat16 [32, 65536, 64], P('tm', 'space'), may hold values from -1.5 to 1.5
- shrinkage: bfloat16 [32, 65536], P('tm', 'space'), may hold values from 1 to 4
- memory_value: bfloat16 [32, 65536, 512], P('tm', 'space'), may hold values from -6 to 6
- block_list: int32 [512, 6], P('space'), may hold values from 0 to 11, as said below
- block_count: int32 [512], P('space'), may hold values from 1 to 6, as said below
Outputs:
- readout: bfloat16 [1, 65536, 512], P(None, 'space')
Inputs may be any that keep to these rules, and one draw needn't show every extreme that they name: `block_list`: entries of a row are distinct; rows of the first tile name no block under 2, rows of the last tile none of 10 or above. `block_count`: the first block of every tile uses all 6 listed blocks.
All inputs are finite; a program needn't handle non-finite values.
Results may differ from a plain program's by a relative error of at most 0.0061.
Values may be sent and summed in bfloat16 or wider, within the bound.
A program may use at most 128 MiB of HBM per device.

v0:
```python
import math

import jax
import jax.numpy as jnp
from jax import lax
from jax.sharding import PartitionSpec as P

BS = 128
W = 2


def padded(x, sides, width):
    for axis, dim in sides:
        size, length = (lax.axis_size(axis), x.shape[dim])
        up = [(i, (i + 1) % size) for i in range(size - 1)]
        down = [(j, i) for i, j in up]
        last = lax.slice_in_dim(x, length - width, length, axis=dim)
        initial = lax.slice_in_dim(x, 0, width, axis=dim)
        before = lax.ppermute(last, axis, up)
        after = lax.ppermute(initial, axis, down)
        x = jnp.concatenate([before, x, after], axis=dim)
    return x


def shards(query_key, selection, memory_key, shrinkage, memory_value, block_list, block_count):
    frames = memory_key.shape[0]
    frames_q = query_key.shape[0]
    pixels = query_key.shape[1]
    key_width = query_key.shape[2]
    value_width = memory_value.shape[2]
    n_blocks = pixels // BS
    n_listed = block_list.shape[1]
    window = n_blocks + 2 * W
    score_scale = 1.0 / math.sqrt(key_width)
    near_key, near_value, near_shrink = (
        padded(memory_key, (("space", 1),), W * BS),
        padded(memory_value, (("space", 1),), W * BS),
        padded(shrinkage, (("space", 1),), W * BS),
    )
    key_square = (near_key.astype(jnp.float32) ** 2).astype(jnp.bfloat16)
    key_blocks = near_key.reshape(frames, window, BS, key_width)
    square_blocks = key_square.reshape(frames, window, BS, key_width)
    value_blocks = near_value.reshape(frames, window, BS, value_width)
    shrink_blocks = near_shrink.reshape(frames, window, BS)
    query_f = query_key.astype(jnp.float32)
    select_f = selection.astype(jnp.float32)
    query_sel = (2.0 * query_f * select_f).astype(jnp.bfloat16)
    self_term = jnp.sum(select_f * query_f * query_f, axis=-1)
    per_step = max((divisor for divisor in (1, 2, 3, 4) if n_blocks % divisor == 0))
    groups = n_blocks // per_step
    query_groups = query_sel.reshape(frames_q, groups, per_step, BS, key_width).transpose(
        1, 2, 0, 3, 4
    )
    select_groups = selection.reshape(frames_q, groups, per_step, BS, key_width).transpose(
        1, 2, 0, 3, 4
    )
    self_groups = self_term.reshape(frames_q, groups, per_step, BS).transpose(1, 2, 0, 3)
    list_groups = block_list.reshape(groups, per_step, n_listed)
    count_groups = block_count.reshape(groups, per_step)

    def score_group(inputs):
        query_grp, select_grp, self_grp, listed = inputs
        squares = jnp.take(square_blocks, listed, axis=1)
        key_rows = jnp.take(key_blocks, listed, axis=1)
        shrink = jnp.take(shrink_blocks, listed, axis=1).astype(jnp.float32).transpose(1, 0, 2, 3)
        quad_term = jnp.einsum(
            "gqrc,fgjnc->gqrfjn", select_grp, squares, preferred_element_type=jnp.float32
        )
        cross_term = jnp.einsum(
            "gqrc,fgjnc->gqrfjn", query_grp, key_rows, preferred_element_type=jnp.float32
        )
        return (
            -shrink[:, None, None]
            * (quad_term - cross_term + self_grp[..., None, None, None])
            * score_scale
        )

    scores = lax.map(score_group, (query_groups, select_groups, self_groups, list_groups))
    usable = (jnp.arange(n_listed, dtype=jnp.int32)[None, None, :] < count_groups[..., None])[
        :, :, None, None, None, :, None
    ]
    local_top = jnp.max(jnp.where(usable, scores, -jnp.inf), axis=(4, 5, 6))

    def read_group(inputs):
        scores_grp, top_grp, usable_grp, listed = inputs
        weights = jnp.where(
            usable_grp,
            jnp.exp(scores_grp - top_grp[..., None, None, None]),
            jnp.zeros_like(scores_grp),
        )
        group_total = jnp.sum(weights, axis=(3, 4, 5))
        values = jnp.take(value_blocks, listed, axis=1)
        group_sum = jnp.einsum(
            "gqrfjn,fgjnv->gqrv",
            weights.astype(jnp.bfloat16),
            values,
            preferred_element_type=jnp.float32,
        )
        return (group_sum, group_total)

    summed, row_total = lax.map(read_group, (scores, local_top, usable, list_groups))
    summed = summed.transpose(2, 0, 1, 3, 4).reshape(frames_q, pixels, value_width)
    row_total = row_total.transpose(2, 0, 1, 3).reshape(frames_q, pixels)
    group_top = local_top.transpose(2, 0, 1, 3).reshape(frames_q, pixels)
    row_top = lax.pmax(group_top, "tm")
    factor = jnp.exp(group_top - row_top)
    summed_all, total_all = lax.psum((summed * factor[..., None], row_total * factor), "tm")
    return (summed_all / total_all[..., None]).astype(jnp.bfloat16)


def solution(mesh):
    in_specs = (
        P(None, "space", None),
        P(None, "space", None),
        P("tm", "space", None),
        P("tm", "space"),
        P("tm", "space", None),
        P("space", None),
        P("space"),
    )
    out_specs = P(None, "space", None)
    return jax.shard_map(shards, mesh=mesh, in_specs=in_specs, out_specs=out_specs, check_vma=False)
```

profile of v0, /device:TPU:2, one launch (start us, length us, event | category | flops | bytes accessed | tf_op | source)
XLA Modules:
  0.0 578.4 jit_solution(8308020960636234133)
XLA Ops:
  6.5 1.0 fusion.35
  7.5 1.9 collective-permute-start.2
  9.5 3.6 collective-permute-start.3
  13.1 0.7 fusion.36
  13.8 1.9 collective-permute-start
  15.7 5.6 collective-permute-start.1
  21.3 3.0 fusion.34
  24.3 1.9 collective-permute-start.4
  26.3 0.7 lt.69
  27.6 1.6 fusion.32
  29.8 1.0 transpose_reshape.9
  30.9 3.6 collective-permute-start.5
  34.6 0.7 maximum_bitcast_fusion
  35.3 1.1 pad_maximum_fusion.1
  36.4 0.9 copy.17
  37.3 1.6 multiply_convert_fusion
  38.9 52.1 %while.22 = (s32[]{:T(128)}, f32[2,4,1,128,4,6,128]{6,3,5,4,1,2,0:T(8,128)}, s32[2,4,6]{2,1,0:T(4,128)}, bf16[4,12,128]{2,0,1:T(4,128)(2,1)S(1)}, bf16[2,4,1,128...) while((s32[]{:T(128)}, ...), condition=%wide.region_2.4_spmd, body=%wide.region_1.3_spmd.sunk | while | flops 410556640 | bytes 41590792 | solution.py:78
  40.1 2.6 gather_fusion
  42.6 2.4 copy.59
  45.1 5.1 fusion.52
  51.7 2.7 gather_fusion.2
  54.4 2.4 copy.61
  57.5 7.5 %bitcast_dynamic-update-slice_fusion.2 = f32[2,4,1,128,4,6,128]{6,3,5,4,1,2,0:T(8,128)} fusion(f32[2,4,1,128,4,6,128]{6,3,5,4,1,2,0:T(8,128)} %get-tuple-element.279, s32[]{:T(128)} %get-tuple-element.278, f32[4,128,4,6,128]{4,1,3,2,0:T(8,128)} %fusion.52, f32[4,128]{1,0:T(4,128)S(1)} %dynamic-slice_bitcast_fusion.6, ...), kind=kOutput, calls=%fused_computation.26.clone.1 | convolution fusion | flops 208404480 | bytes 14273048 | tf_op jit(solution)/shard_map/while/body/eval_jaxpr/gqrc,fgjnc->gqrfjn/dot_general | solution.py:69
  65.0 0.7 compare_and_fusion.4
  66.1 2.6 gather_fusion
  68.7 2.4 copy.59
  71.2 5.0 fusion.52
  77.7 2.7 gather_fusion.2
  80.4 2.4 copy.61
  83.5 7.4 %bitcast_dynamic-update-slice_fusion.2 = f32[2,4,1,128,4,6,128]{6,3,5,4,1,2,0:T(8,128)} fusion(f32[2,4,1,128,4,6,128]{6,3,5,4,1,2,0:T(8,128)} %get-tuple-element.279, s32[]{:T(128)} %get-tuple-element.278, f32[4,128,4,6,128]{4,1,3,2,0:T(8,128)} %fusion.52, f32[4,128]{1,0:T(4,128)S(1)} %dynamic-slice_bitcast_fusion.6, ...), kind=kOutput, calls=%fused_computation.26.clone.1 | convolution fusion | flops 208404480 | bytes 14273048 | tf_op jit(solution)/shard_map/while/body/eval_jaxpr/gqrc,fgjnc->gqrfjn/dot_general | solution.py:69
  91.0 5.6 select_reduce_fusion
  96.5 47.8 %pmax.7 = f32[1,1024]{1,0:T(1,128)S(1)} all-reduce(f32[1,1024]{1,0:T(1,128)S(1)} %bitcast.147), channel_id=1, replica_groups=mesh['space'=64,'tm'=8] {'tm'}, use_global_device_ids=true, to_apply=%region_7.9 | all-reduce | flops 1024 | bytes 8192 | tf_op jit(solution)/shard_map/pmax | solution.py:105
  144.4 6.0 %pad_maximum_fusion = bf16[4,1536,512]{2,1,0:T(8,128)(2,1)} fusion(bf16[4,256,512]{2,1,0:T(8,128)(2,1)} %collective-permute-done.5, bf16[4,1024,512]{2,1,0:T(8,128)(2,1)} %param.17, bf16[4,256,512]{2,1,0:T(8,128)(2,1)} %collective-permute-done.4), kind=kLoop, calls=%fused_computation.50 | loop fusion | flops 18874368 | bytes 12582912 | tf_op jit(solution)/shard_map/concatenate | solution.py:21
  150.4 42.9 %while.23 = (s32[]{:T(128)}, f32[2,4,1,128,512]{4,3,1,2,0:T(8,128)S(1)}, f32[2,4,1,128]{3,2,1,0:T(1,128)S(1)}, pred[2,4,1,1,1,6,1]{5,1,6,4,3,2,0:T(4,128)(4,1)S(...) while((s32[]{:T(128)}, ...), condition=%wide.region_6.8_spmd, body=%wide.region_4.7_spmd.sunk | while | flops 1626342144 | bytes 101733264 | solution.py:101
  150.4 0.7 compare_select_fusion.8
  151.2 8.8 %gather_fusion.3 = bf16[24,4,128,512]{3,2,1,0:T(8,128)(2,1)} fusion(bf16[4,12,128,512]{3,2,1,0:T(8,128)(2,1)} %get-tuple-element.323, s32[1024]{0:T(1024)S(1)} %pad_clamp_fusion.8), kind=kCustom, calls=%fused_computation.1.clone.1 | custom fusion | bytes 25165920 | tf_op jit(solution)/shard_map/while/body/eval_jaxpr/jit(_take)/gather | solution.py:92
  160.7 8.2 %fusion.57 = f32[2,4,1,128,512]{4,3,1,2,0:T(8,128)S(1)} fusion(f32[2,4,1,128,512]{4,3,1,2,0:T(8,128)S(1)} %get-tuple-element.308, s32[]{:T(128)} %get-tuple-element.307, bf16[4,6,4,128,512]{4,3,2,1,0:T(8,128)(2,1)} %bitcast.139, pred[4,6]{1,0:T(4,128)(4,1)S(1)} %compare_and_fusion.5, f32[2,4,1,128,4,6,128]{6,3,5,4,1,2,0:T(8,128)} %get-tuple-element.320, ...), kind=kOutput, calls=%fused_computation.18.clone.1 | convolution fusion | flops 1621622784 | bytes 19927040 | tf_op jit(solution)/shard_map/while/body/eval_jaxpr/gqrfjn,fgjnv->gqrv/dot_general | solution.py:93
  168.9 1.8 copy-done.2
  170.7 1.2 fusion.58
  171.9 0.7 compare_select_fusion.8
  172.7 8.8 %gather_fusion.3 = bf16[24,4,128,512]{3,2,1,0:T(8,128)(2,1)} fusion(bf16[4,12,128,512]{3,2,1,0:T(8,128)(2,1)} %get-tuple-element.323, s32[1024]{0:T(1024)S(1)} %pad_clamp_fusion.8), kind=kCustom, calls=%fused_computation.1.clone.1 | custom fusion | bytes 25165920 | tf_op jit(solution)/shard_map/while/body/eval_jaxpr/jit(_take)/gather | solution.py:92
  182.1 8.2 %fusion.57 = f32[2,4,1,128,512]{4,3,1,2,0:T(8,128)S(1)} fusion(f32[2,4,1,128,512]{4,3,1,2,0:T(8,128)S(1)} %get-tuple-element.308, s32[]{:T(128)} %get-tuple-element.307, bf16[4,6,4,128,512]{4,3,2,1,0:T(8,128)(2,1)} %bitcast.139, pred[4,6]{1,0:T(4,128)(4,1)S(1)} %compare_and_fusion.5, f32[2,4,1,128,4,6,128]{6,3,5,4,1,2,0:T(8,128)} %get-tuple-element.320, ...), kind=kOutput, calls=%fused_computation.18.clone.1 | convolution fusion | flops 1621622784 | bytes 19927040 | tf_op jit(solution)/shard_map/while/body/eval_jaxpr/gqrfjn,fgjnv->gqrv/dot_general | solution.py:93
  190.3 1.8 copy-done.2
  192.1 1.2 fusion.58
  193.4 1.5 broadcast_multiply_fusion
  194.9 41.1 %psum.15 = f32[1024]{0:T(1024)S(1)} all-reduce(f32[1024]{0:T(1024)S(1)} %bitcast.152), channel_id=1, replica_groups=mesh['space'=64,'tm'=8] {'tm'}, use_global_device_ids=true, to_apply=%region_9.11 | all-reduce | flops 1024 | bytes 8192 | tf_op jit(solution)/shard_map/psum | solution.py:107
  236.0 332.8 %all-reduce.2.cloned.1.call-done = f32[1,1024,512]{2,1,0:T(8,128)} async-done(((f32[1,1024,512]{2,1,0:T(8,128)}), f32[1,1024,512]{2,1,0:T(8,128)}) %all-reduce.2.cloned.1.call-update) | async-done | bytes 2097168 | tf_op jit(solution)/shard_map/psum | solution.py:107
  568.8 2.8 divide_convert_fusion
  (68 shorter events, 9.0 us)
Async XLA Ops:
  6.5 562.3 %all-reduce.2.cloned.1.call-start = ((), (), s32[]{:S(2)}) async-start(), calls=%async_computation | async-start | bytes 4194304 | tf_op jit(solution)/shard_map/psum | solution.py:107
  7.5 27.8 %collective-permute-start.2 = (bf16[4,256,64]{1,2,0:T(8,128)(2,1)S(1)}, bf16[4,256,64]{1,2,0:T(8,128)(2,1)S(1)}, u32[]{:S(2)}, u32[]{:S(2)}) collective-permute-start(bf16[4,256,64]{1,2,0:T(8,128)(2,1)S(1)} %get-tuple-element.150), channel_id=1, source_target_pairs={{0,8},{8,16},{16,24},{24,32},{32,40},{40,48},{48,56},{56,64},{64,7... | collective-permute-start | bytes 393224 | tf_op jit(solution)/shard_map/ppermute | solution.py:19
  9.5 25.8 %collective-permute-start.3 = (bf16[4,256,64]{1,2,0:T(8,128)(2,1)S(1)}, bf16[4,256,64]{1,2,0:T(8,128)(2,1)S(1)}, u32[]{:S(2)}, u32[]{:S(2)}) collective-permute-start(bf16[4,256,64]{1,2,0:T(8,128)(2,1)S(1)} %get-tuple-element.151), channel_id=1, source_target_pairs={{8,0},{16,8},{24,16},{32,24},{40,32},{48,40},{56,48},{64,56},{72,6... | collective-permute-start | bytes 393224 | tf_op jit(solution)/shard_map/ppermute | solution.py:20
  13.8 17.1 %collective-permute-start = (bf16[4,256]{1,0:T(4,128)(2,1)S(1)}, bf16[4,256]{1,0:T(4,128)(2,1)S(1)}, u32[]{:S(2)}, u32[]{:S(2)}) collective-permute-start(bf16[4,256]{1,0:T(4,128)(2,1)S(1)} %get-tuple-element.154), channel_id=1, source_target_pairs={{0,8},{8,16},{16,24},{24,32},{32,40},{40,48},{48,56},{56,64},{64,7... | collective-permute-start | bytes 6152 | tf_op jit(solution)/shard_map/ppermute | solution.py:19
  15.7 18.9 %collective-permute-start.1 = (bf16[4,256]{1,0:T(4,128)(2,1)S(1)}, bf16[4,256]{1,0:T(4,128)(2,1)S(1)}, u32[]{:S(2)}, u32[]{:S(2)}) collective-permute-start(bf16[4,256]{1,0:T(4,128)(2,1)S(1)} %get-tuple-element.155), channel_id=1, source_target_pairs={{8,0},{16,8},{24,16},{32,24},{40,32},{48,40},{56,48},{64,56},{72,6... | collective-permute-start | bytes 6152 | tf_op jit(solution)/shard_map/ppermute | solution.py:20
  24.3 120.1 %collective-permute-start.4 = (bf16[4,256,512]{2,1,0:T(8,128)(2,1)}, bf16[4,256,512]{2,1,0:T(8,128)(2,1)}, u32[]{:S(2)}, u32[]{:S(2)}) collective-permute-start(bf16[4,256,512]{2,1,0:T(8,128)(2,1)} %get-tuple-element.148), channel_id=1, source_target_pairs={{0,8},{8,16},{16,24},{24,32},{32,40},{40,48},{48,56},{56,64},{64,7... | collective-permute-start | bytes 3145736 | tf_op jit(solution)/shard_map/ppermute | solution.py:19
  30.9 113.5 %collective-permute-start.5 = (bf16[4,256,512]{2,1,0:T(8,128)(2,1)}, bf16[4,256,512]{2,1,0:T(8,128)(2,1)}, u32[]{:S(2)}, u32[]{:S(2)}) collective-permute-start(bf16[4,256,512]{2,1,0:T(8,128)(2,1)} %get-tuple-element.149), channel_id=1, source_target_pairs={{8,0},{16,8},{24,16},{32,24},{40,32},{48,40},{56,48},{64,56},{72,6... | collective-permute-start | bytes 3145736 | tf_op jit(solution)/shard_map/ppermute | solution.py:20
  38.9 1.2 copy-start
  40.1 10.1 %copy-start.4 = (s32[1024]{0:T(1024)}, s32[1024]{0:T(1024)S(1)}, u32[]{:S(2)}) copy-start(s32[1024]{0:T(1024)S(1)} %pad_clamp_fusion.6) | copy-start | bytes 12292 | tf_op jit(solution)/shard_map/while
  57.5 7.5 %copy-start.1 = (bf16[4,12,128,64]{3,2,1,0:T(8,128)(2,1)S(1)}, bf16[4,12,128,64]{3,2,1,0:T(8,128)(2,1)}, u32[]{:S(2)}) copy-start(bf16[4,12,128,64]{3,2,1,0:T(8,128)(2,1)} %copy-done) | copy-start | bytes 2359300 | tf_op jit(solution)/shard_map/while
  65.0 1.2 copy-start
  66.1 10.1 %copy-start.4 = (s32[1024]{0:T(1024)}, s32[1024]{0:T(1024)S(1)}, u32[]{:S(2)}) copy-start(s32[1024]{0:T(1024)S(1)} %pad_clamp_fusion.6) | copy-start | bytes 12292 | tf_op jit(solution)/shard_map/while
  83.5 7.5 %copy-start.1 = (bf16[4,12,128,64]{3,2,1,0:T(8,128)(2,1)S(1)}, bf16[4,12,128,64]{3,2,1,0:T(8,128)(2,1)}, u32[]{:S(2)}) copy-start(bf16[4,12,128,64]{3,2,1,0:T(8,128)(2,1)} %copy-done) | copy-start | bytes 2359300 | tf_op jit(solution)/shard_map/while
  144.4 6.1 %copy-start.3 = (f32[2,4,1,128,512]{4,3,1,2,0:T(8,128)S(1)}, f32[2,4,1,128,512]{4,3,1,2,0:T(8,128)}, u32[]{:S(2)}) copy-start(f32[2,4,1,128,512]{4,3,1,2,0:T(8,128)} %custom-call.9) | copy-start | bytes 6291460
  144.4 6.1 %copy-start.5 = (f32[2,4,1,128]{3,2,1,0:T(1,128)S(1)}, f32[2,4,1,128]{3,2,1,0:T(1,128)}, u32[]{:S(2)}) copy-start(f32[2,4,1,128]{3,2,1,0:T(1,128)} %custom-call.10) | copy-start | bytes 12292
  144.4 6.1 %copy-start.6 = (pred[2,4,1,1,1,6,1]{5,1,6,4,3,2,0:T(4,128)(4,1)S(1)}, pred[2,4,1,1,1,6,1]{5,1,6,4,3,2,0:T(4,128)(4,1)}, u32[]{:S(2)}) copy-start(pred[2,4,1,1,1,6,1]{5,1,6,4,3,2,0:T(4,128)(4,1)} %iota_compare_fusion.1) | copy-start | bytes 148
  160.7 10.0 %copy-start.2 = (f32[2,4,1,128,4,6,128]{6,3,5,4,1,2,0:T(8,128)S(1)}, f32[2,4,1,128,4,6,128]{6,3,5,4,1,2,0:T(8,128)}, u32[]{:S(2)}) copy-start(f32[2,4,1,128,4,6,128]{6,3,5,4,1,2,0:T(8,128)} %get-tuple-element.320) | copy-start | bytes 37748740 | tf_op jit(solution)/shard_map/while
  182.1 10.0 %copy-start.2 = (f32[2,4,1,128,4,6,128]{6,3,5,4,1,2,0:T(8,128)S(1)}, f32[2,4,1,128,4,6,128]{6,3,5,4,1,2,0:T(8,128)}, u32[]{:S(2)}) copy-start(f32[2,4,1,128,4,6,128]{6,3,5,4,1,2,0:T(8,128)} %get-tuple-element.320) | copy-start | bytes 37748740 | tf_op jit(solution)/shard_map/while
Sparse Core Ops, SparseCore 0:
  195.0 373.7 all-reduce.1
where the time goes:
time: 580 us; the launch traced here: 578 us
  waiting for transfers between devices  333 us (57%)
  blocking collectives  88.9 us (15%)
  local copies, waits for them, and re-layouts  52.7 us (9%)
  matrix products  41.4 us (7%)
  other arithmetic  30.2 us (5%)
  starting transfers between devices  18.6 us (3%)
  between operations  13.6 us (2%)
    psum x1, waiting for transfers between devices, shards(): lax.psum((summed * factor[..., None], row_total * factor), 'tm')  333 us
    pmax x1, blocking collectives, shards(): row_top = lax.pmax(group_top, 'tm')  47.8 us
    psum x1, blocking collectives, shards(): lax.psum((summed * factor[..., None], row_total * factor), 'tm')  41.1 us
    gather x2, local copies, waits for them, and re-layouts, read_group(): values = jnp.take(value_blocks, listed, axis=1)  17.6 us
    dot_general x2, matrix products, read_group(): jnp.einsum('gqrfjn,fgjnv->gqrv', weights.astype(jnp.bfloat16), values, pr...  16.4 us
    dot_general x2, matrix products, score_group(): jnp.einsum('gqrc,fgjnc->gqrfjn', query_grp, key_rows, preferred_element_t...  14.9 us
    ppermute x3, starting transfers between devices, padded(): after = lax.ppermute(initial, axis, down)  12.9 us
  transfers between devices with their start and end apart: 7, of which 1 were waited for; matrix products, arithmetic and copies ran while one was open for 12% of the time, Pallas kernels for 0%

commit v1 on v0

v1 whole, which is shorter than its diff:
```python
import functools
import math

import jax
import jax.numpy as jnp
from jax import lax
from jax.experimental import pallas as pl
from jax.experimental.pallas import tpu as pltpu
from jax.sharding import PartitionSpec as P

BS = 128
W = 2
NY = 4
NZ = 2
HALVES = 2
LAG_Z = 6
NEG = -1e30
MESH = pl.DeviceIdType.MESH


def kernel(
    n_space, list_ref, count_ref, query_ref, select_ref, shrink_ref, key_hbm, value_hbm, out_ref,
    key_raw, key_cat, shrink_win, value_lo, value_hi, weights, scores, tops, scales,
    lse_own, lse_all, part, part_in, zsum, zin,
    own_sem, halo_send, halo_recv, lse_send, lse_recv, y_send, y_recv, z_send, z_recv, g_send, g_recv,
):
    frames, n_blocks = key_hbm.shape[0], key_hbm.shape[1]
    n_listed = list_ref.shape[1]
    ck = key_hbm.shape[3]
    cols = value_hbm.shape[3] // HALVES
    pieces = HALVES * n_blocks
    group = frames * BS
    n_tm = NY * NZ
    scale = 1.0 / math.sqrt(ck)

    s = lax.axis_index("space")
    t = lax.axis_index("tm")
    y, zh = t // NZ, lax.rem(t, NZ)
    has_up, has_down = s < n_space - 1, s > 0
    values = (value_lo, value_hi)

    own = [pltpu.make_async_copy(key_hbm, key_raw.at[:, pl.ds(W, n_blocks)], own_sem.at[0])]
    for h in range(HALVES):
        own.append(
            pltpu.make_async_copy(
                value_hbm.at[:, :, :, pl.ds(h * cols, cols)],
                values[h].at[:, pl.ds(W, n_blocks)],
                own_sem.at[1 + h],
            )
        )
    for copy in own:
        copy.start()
    for b in range(n_blocks):
        shrink_win[W + b, 0:frames, :] = shrink_ref[:, b * BS : (b + 1) * BS].astype(jnp.float32) * (-scale)

    @pl.when(jnp.logical_not(has_down))
    def _():
        key_raw[:, 0:W] = jnp.zeros_like(key_raw[:, 0:W])
        shrink_win[0:W] = jnp.zeros_like(shrink_win[0:W])
        for v in values:
            v[:, 0:W] = jnp.zeros_like(v[:, 0:W])

    @pl.when(jnp.logical_not(has_up))
    def _():
        key_raw[:, W + n_blocks :] = jnp.zeros_like(key_raw[:, W + n_blocks :])
        shrink_win[W + n_blocks :] = jnp.zeros_like(shrink_win[W + n_blocks :])
        for v in values:
            v[:, W + n_blocks :] = jnp.zeros_like(v[:, W + n_blocks :])

    barrier = pltpu.get_barrier_semaphore()

    def peer(k):
        return (s, lax.rem(t + k, n_tm))

    def y_peer(k):
        return (s, lax.rem(y + k, NY) * NZ + zh)

    z_peer = (s, y * NZ + (1 - zh))
    for k in range(1, n_tm):
        pl.semaphore_signal(barrier, inc=1, device_id=peer(k), device_id_type=MESH)

    @pl.when(has_up)
    def _():
        pl.semaphore_signal(barrier, inc=1, device_id=(s + 1, t), device_id_type=MESH)

    @pl.when(has_down)
    def _():
        pl.semaphore_signal(barrier, inc=1, device_id=(s - 1, t), device_id_type=MESH)

    @pl.when(jnp.logical_and(has_up, has_down))
    def _():
        pl.semaphore_wait(barrier, n_tm + 1)

    @pl.when(jnp.logical_not(jnp.logical_and(has_up, has_down)))
    def _():
        pl.semaphore_wait(barrier, n_tm)

    def remote(src, dst, send, recv, to):
        return pltpu.make_async_remote_copy(
            src_ref=src, dst_ref=dst, send_sem=send, recv_sem=recv, device_id=to, device_id_type=MESH
        )

    top_blocks, low_blocks = pl.ds(n_blocks - W, W), pl.ds(0, W)
    ups, downs = [], []
    for halo, (blocks, dst_at, to) in (
        (ups, (top_blocks, pl.ds(0, W), (s + 1, t))),
        (downs, (low_blocks, pl.ds(W + n_blocks, W), (s - 1, t))),
    ):
        d = 0 if halo is ups else 1
        own_at = pl.ds(n_blocks, W) if halo is ups else pl.ds(W, W)
        halo.append(remote(key_hbm.at[:, blocks], key_raw.at[:, dst_at], halo_send.at[d, 0], halo_recv.at[d, 0], to))
        halo.append(remote(shrink_win.at[own_at], shrink_win.at[dst_at], halo_send.at[d, 1], halo_recv.at[d, 1], to))
        for h in range(HALVES):
            halo.append(
                remote(
                    value_hbm.at[:, blocks, :, pl.ds(h * cols, cols)],
                    values[h].at[:, dst_at],
                    halo_send.at[d, 2 + h],
                    halo_recv.at[d, 2 + h],
                    to,
                )
            )

    @pl.when(has_up)
    def _():
        for copy in ups:
            copy.start()

    @pl.when(has_down)
    def _():
        for copy in downs:
            copy.start()

    def halo_arrived(n):
        @pl.when(has_down)
        def _():
            ups[n].wait_recv()

        @pl.when(has_up)
        def _():
            downs[n].wait_recv()

    def widen(at):
        k = key_raw[:, at]
        kf = k.astype(jnp.float32)
        key_cat[:, at] = jnp.concatenate([(kf * kf).astype(jnp.bfloat16), k], axis=-1)

    own[0].wait()

    @pl.loop(0, n_blocks)
    def _(b):
        widen(W + b)

    halo_arrived(0)
    halo_arrived(1)
    for w in (0, 1, W + n_blocks, W + n_blocks + 1):
        widen(w)

    def lse_copy(k, b):
        return remote(lse_own.at[b], lse_all.at[t, b], lse_send.at[k, b], lse_recv.at[k, b], peer(k))

    @pl.loop(0, n_blocks)
    def _(b):
        rows = pl.ds(pl.multiple_of(b * BS, BS), BS)
        q = query_ref[0, rows, :].astype(jnp.float32)
        sel = select_ref[0, rows, :]
        sel_f = sel.astype(jnp.float32)
        self_term = jnp.sum(sel_f * q * q, axis=1, keepdims=True)
        lhs = jnp.concatenate([sel, -((2.0 * q * sel_f).astype(jnp.bfloat16))], axis=1)
        live = jnp.full((1, group), count_ref[b], jnp.int32)
        best = jnp.full((BS, BS), NEG, jnp.float32)
        for j in range(n_listed):
            w = list_ref[b, j]
            rhs = jnp.concatenate([key_cat[f, w] for f in range(frames)], axis=0)
            near = shrink_win[w]
            factor = jnp.concatenate([near[f : f + 1] for f in range(frames)], axis=1)
            dots = lax.dot_general(lhs, rhs, (((1,), (1,)), ((), ())), preferred_element_type=jnp.float32)
            score = jnp.where(live > j, (dots + self_term) * factor, NEG)
            scores[j] = score
            for f in range(frames):
                best = jnp.maximum(best, score[:, f * BS : (f + 1) * BS])
        top = jnp.max(best, axis=1, keepdims=True)
        total = jnp.zeros((BS, BS), jnp.float32)
        for j in range(n_listed):
            p = jnp.exp(scores[j] - top)
            weights[b, :, j * group : (j + 1) * group] = p.astype(jnp.bfloat16)
            for f in range(frames):
                total = total + p[:, f * BS : (f + 1) * BS]
        lse = top + jnp.log(jnp.sum(total, axis=1, keepdims=True))
        tops[b] = jnp.broadcast_to(top, (BS, BS))
        row = jnp.broadcast_to(lse, (BS, BS)).T[0:1, :]
        lse_own[b] = row
        lse_all[t, b] = row
        for k in range(1, n_tm):
            lse_copy(k, b).start()

    def lse_arrival(k, b):
        at = lse_all.at[lax.rem(t + n_tm - k, n_tm), b]
        return remote(lse_own.at[b], at, lse_send.at[k, b], lse_recv.at[k, b], peer(k))

    def y_copy(k, i):
        return remote(part.at[i, lax.rem(y + k, NY)], part_in.at[k - 1, i], y_send.at[k - 1, i], y_recv.at[k - 1, i], y_peer(k))

    def z_copy(i):
        return remote(zsum.at[i], zin.at[i], z_send.at[i], z_recv.at[i], z_peer)

    def g_copy(k, i):
        return remote(out_ref.at[i, y], out_ref.at[i, y], g_send.at[k - 1, i], g_recv.at[k - 1, i], y_peer(k))

    def g_arrival(k, i):
        at = out_ref.at[i, lax.rem(y + NY - k, NY)]
        return remote(out_ref.at[i, y], at, g_send.at[k - 1, i], g_recv.at[k - 1, i], y_peer(k))

    def stage_value(h, b):
        i = h * n_blocks + b
        acc = jnp.zeros((BS, cols), jnp.float32)
        for j in range(n_listed):
            w = list_ref[b, j]
            rhs = jnp.concatenate([values[h][f, w] for f in range(frames)], axis=0)
            acc = acc + jnp.dot(
                weights[b, :, j * group : (j + 1) * group], rhs, preferred_element_type=jnp.float32
            )
        if h == 0:
            for k in range(1, n_tm):
                lse_arrival(k, b).wait_recv()
            ls = lse_all[:, b]
            peak = jnp.max(ls, axis=0)
            whole = peak + jnp.log(jnp.sum(jnp.exp(ls - peak[None]), axis=0))
            scales[b] = jnp.exp(tops[b] - jnp.broadcast_to(whole, (BS, BS)).T)
        factor = jnp.concatenate([scales[b]] * (cols // BS), axis=1)
        part[i] = (acc * factor).astype(jnp.bfloat16).reshape(NY, BS // NY, cols)
        for k in range(1, NY):
            y_copy(k, i).start()

    def stage_y(i):
        total = part[i, y].astype(jnp.float32)
        for k in range(1, NY):
            y_copy(k, i).wait_recv()
            total = total + part_in[k - 1, i].astype(jnp.float32)
        zsum[i] = total.astype(jnp.bfloat16)
        z_copy(i).start()

    def stage_z(i):
        z_copy(i).wait_recv()
        out_ref[i, y] = (zsum[i].astype(jnp.float32) + zin[i].astype(jnp.float32)).astype(jnp.bfloat16)
        for k in range(1, NY):
            g_copy(k, i).start()

    for h in range(HALVES):
        own[1 + h].wait()
        halo_arrived(2 + h)

        @pl.loop(0, n_blocks)
        def _(b):
            i = h * n_blocks + b
            stage_value(h, b)

            @pl.when(i >= 1)
            def _():
                stage_y(i - 1)

            @pl.when(i >= LAG_Z)
            def _():
                stage_z(i - LAG_Z)

    stage_y(pieces - 1)

    @pl.loop(pieces - LAG_Z, pieces)
    def _(i):
        stage_z(i)

    @pl.loop(0, pieces)
    def _(i):
        for k in range(1, NY):
            g_arrival(k, i).wait_recv()
            y_copy(k, i).wait_send()
            g_copy(k, i).wait_send()
        z_copy(i).wait_send()

    @pl.loop(0, n_blocks)
    def _(b):
        for k in range(1, n_tm):
            lse_copy(k, b).wait_send()

    @pl.when(has_up)
    def _():
        for copy in ups:
            copy.wait_send()

    @pl.when(has_down)
    def _():
        for copy in downs:
            copy.wait_send()


def shards(n_space, query_key, selection, memory_key, shrinkage, memory_value, block_list, block_count):
    frames, pixels, ck = memory_key.shape
    cv = memory_value.shape[2]
    n_blocks = pixels // BS
    n_listed = block_list.shape[1]
    window = n_blocks + 2 * W
    cols = cv // HALVES
    pieces = HALVES * n_blocks
    n_tm = NY * NZ
    part_rows = BS // NY
    bf, f32 = jnp.bfloat16, jnp.float32
    keys = memory_key.reshape(frames, n_blocks, BS, ck)
    vals = memory_value.reshape(frames, n_blocks, BS, cv)
    vmem = pl.BlockSpec(memory_space=pltpu.VMEM)
    smem = pl.BlockSpec(memory_space=pltpu.SMEM)
    hbm = pl.BlockSpec(memory_space=pltpu.HBM)
    dma = pltpu.SemaphoreType.DMA
    out = pl.pallas_call(
        functools.partial(kernel, n_space),
        out_shape=jax.ShapeDtypeStruct((pieces, NY, part_rows, cols), bf),
        in_specs=[smem, smem, vmem, vmem, vmem, hbm, hbm],
        out_specs=vmem,
        scratch_shapes=[
            pltpu.VMEM((frames, window, BS, ck), bf),
            pltpu.VMEM((frames, window, BS, 2 * ck), bf),
            pltpu.VMEM((window, 8, BS), f32),
            pltpu.VMEM((frames, window, BS, cols), bf),
            pltpu.VMEM((frames, window, BS, cols), bf),
            pltpu.VMEM((n_blocks, BS, n_listed * frames * BS), bf),
            pltpu.VMEM((n_listed, BS, frames * BS), f32),
            pltpu.VMEM((n_blocks, BS, BS), f32),
            pltpu.VMEM((n_blocks, BS, BS), f32),
            pltpu.VMEM((n_blocks, 1, BS), f32),
            pltpu.VMEM((n_tm, n_blocks, 1, BS), f32),
            pltpu.VMEM((pieces, NY, part_rows, cols), bf),
            pltpu.VMEM((NY - 1, pieces, part_rows, cols), bf),
            pltpu.VMEM((pieces, part_rows, cols), bf),
            pltpu.VMEM((pieces, part_rows, cols), bf),
            dma((1 + HALVES,)),
            dma((2, 2 + HALVES)),
            dma((2, 2 + HALVES)),
            dma((n_tm, n_blocks)),
            dma((n_tm, n_blocks)),
            dma((NY - 1, pieces)),
            dma((NY - 1, pieces)),
            dma((pieces,)),
            dma((pieces,)),
            dma((NY - 1, pieces)),
            dma((NY - 1, pieces)),
        ],
        compiler_params=pltpu.CompilerParams(
            collective_id=0, has_side_effects=True, vmem_limit_bytes=48 << 20
        ),
    )(block_list, block_count, query_key, selection, shrinkage, keys, vals)
    out = out.reshape(HALVES, pixels, cols).transpose(1, 0, 2)
    return out.reshape(1, pixels, cv)


def solution(mesh):
    in_specs = (
        P(None, "space", None),
        P(None, "space", None),
        P("tm", "space", None),
        P("tm", "space"),
        P("tm", "space", None),
        P("space", None),
        P("space"),
    )
    out_specs = P(None, "space", None)
    return jax.shard_map(
        functools.partial(shards, mesh.shape["space"]),
        mesh=mesh,
        in_specs=in_specs,
        out_specs=out_specs,
        check_vma=False,
    )
```

time: 580 us -> 97.8 us (0.17)
  the two profiles are of different devices: /device:TPU:2 before, /device:TPU:32 now
where the time goes in v1:
time: 97.8 us; the launch traced here: 97.5 us
  Pallas kernels  89.2 us (91%)
  local copies, waits for them, and re-layouts  8.27 us (8%)
    pallas_call x1, Pallas kernels, shards(): pl.pallas_call(functools.partial(kernel, n_space), out_shape=jax.ShapeDty...  89.2 us
    unnamed x9, local copies, waits for them, and re-layouts  5.7 us

profile of v1, /device:TPU:32, one launch (start us, length us, event | category | flops | bytes accessed | tf_op | source)
XLA Modules:
  0.0 97.5 jit_solution(8002749968242858447)
XLA Ops:
  0.0 1.1 %copy.9.query_ref = bf16[1,1024,64]{2,1,0:T(8,128)(2,1)S(1)} copy(bf16[1,1024,64]{1,2,0:T(8,128)(2,1)} %param.7) | data formatting | bytes 262144 | tf_op args[0]
  1.1 1.1 %copy.10.select_ref = bf16[1,1024,64]{2,1,0:T(8,128)(2,1)S(1)} copy(bf16[1,1024,64]{1,2,0:T(8,128)(2,1)} %param.8) | data formatting | bytes 262144 | tf_op args[1]
  2.2 1.5 %copy.8 = bf16[4,1024,64]{2,1,0:T(8,128)(2,1)S(1)} copy(bf16[4,1024,64]{1,2,0:T(8,128)(2,1)} %param.9) | data formatting | bytes 1048576 | tf_op args[2]
  3.7 0.0 copy-start
  3.7 0.7 copy-done
  4.4 0.0 copy-start.1
  4.4 0.7 copy-done.1
  5.1 0.0 copy-start.2
  5.1 0.7 copy-done.2
  5.7 89.2 %shard_map.73 = bf16[16,4,32,256]{3,2,1,0:T(8,128)(2,1)S(1)} custom-call(s32[8,6]{1,0:T(8,128)S(1)} %copy-done.1, s32[8]{0:T(128)S(1)} %copy-done.2, bf16[1,1024,64]{2,1,0:T(8,128)(2,1)S(1)} %copy.9.query_ref, bf16[1,1024,64]{2,1,0:T(8,128)(2,1)S(1)} %copy.10.select_ref, bf16[4,1024]{1,0:T(4,128)(2,1)S(1)} %copy-done, bf16[4,8,128,64]{3,2,1,0:T(8,128)(2,1)S(1)} %bitcast.6, ...), custom_call_target="tpu_custom_call" | custom-call | tf_op jit(solution)/shard_map/pallas_call | solution.py:313
  94.9 1.1 %copy.11 = bf16[1024,2,256]{2,1,0:T(2,128)(2,1)S(1)} copy(bf16[1024,2,256]{2,0,1:T(8,128)(2,1)S(1)} %bitcast.5) | data formatting | bytes 2097152 | tf_op jit(solution)/shard_map/transpose | solution.py:350
  96.0 1.5 %reshape.15 = bf16[1,1024,512]{2,1,0:T(8,128)(2,1)} reshape(bf16[1024,2,256]{2,1,0:T(2,128)(2,1)S(1)} %copy.11) | data formatting | bytes 2097152 | tf_op jit(solution)/shard_map/reshape | solution.py:351
Async XLA Ops:
  3.7 0.7 copy-start
  4.4 0.7 copy-start.1
  5.1 0.7 copy-start.2

commit v2 on v1

v2 whole, which is shorter than its diff:
```python
import functools
import math

import jax
import jax.numpy as jnp
from jax import lax
from jax.experimental import pallas as pl
from jax.experimental.pallas import tpu as pltpu
from jax.sharding import PartitionSpec as P

BS = 128
W = 2
NY = 4
NZ = 2
HALVES = 2
LAG_Y = 6
LAG_Z = 7
N_COPIES = 4
NEG = -1e30
MESH = pl.DeviceIdType.MESH


def kernel(
    n_space, list_ref, count_ref, query_hbm, select_hbm, shrink_ref, key_hbm, value_hbm, out_ref,
    query_ref, select_ref, lhs_all, self_all, key_raw, key_cat, shrink_win, value_lo, value_hi, weights, scores, inverse,
    lse_y, lse_z, turned, share_y, share_z, part, part_in, zsum, zin,
    own_sem, halo_send, halo_recv, ly_send, ly_recv, lz_send, lz_recv, y_send, y_recv, z_send, z_recv, g_send, g_recv,
):
    frames, ck = key_hbm.shape[0], key_hbm.shape[1]
    n_blocks, n_listed = list_ref.shape
    n_own, n_halo = n_blocks * BS, W * BS
    cols = value_hbm.shape[3] // HALVES
    pieces = HALVES * n_blocks
    group = frames * BS
    rows_y = BS // NY
    scale = math.log2(math.e) / math.sqrt(ck)

    s = lax.axis_index("space")
    t = lax.axis_index("tm")
    y, zh = t // NZ, lax.rem(t, NZ)
    has_up, has_down = s < n_space - 1, s > 0
    values = (value_lo, value_hi)

    own = [pltpu.make_async_copy(key_hbm, key_raw.at[:, :, pl.ds(n_halo, n_own)], own_sem.at[0])]
    for h in range(HALVES):
        own.append(
            pltpu.make_async_copy(
                value_hbm.at[:, :, :, pl.ds(h * cols, cols)],
                values[h].at[:, pl.ds(W, n_blocks)],
                own_sem.at[1 + h],
            )
        )
    own[0].start()
    queries = [
        pltpu.make_async_copy(query_hbm, query_ref, own_sem.at[1 + HALVES]),
        pltpu.make_async_copy(select_hbm, select_ref, own_sem.at[2 + HALVES]),
    ]
    for copy in queries:
        copy.start()
    def shrink_own(b):
        near = shrink_ref[:, b * BS : (b + 1) * BS].astype(jnp.float32) * (-scale)
        shrink_win[W + b] = jnp.concatenate([near[f : f + 1] for f in range(frames)], axis=1)

    for b in range(n_blocks):
        shrink_own(b)

    @pl.when(jnp.logical_not(has_down))
    def _():
        key_raw[:, :, 0:n_halo] = jnp.zeros((frames, ck, n_halo), key_raw.dtype)
        shrink_win[0:W] = jnp.zeros_like(shrink_win[0:W])
        for v in values:
            v[:, 0:W] = jnp.zeros_like(v[:, 0:W])

    @pl.when(jnp.logical_not(has_up))
    def _():
        key_raw[:, :, n_halo + n_own :] = jnp.zeros((frames, ck, n_halo), key_raw.dtype)
        shrink_win[W + n_blocks :] = jnp.zeros_like(shrink_win[W + n_blocks :])
        for v in values:
            v[:, W + n_blocks :] = jnp.zeros_like(v[:, W + n_blocks :])

    barrier = pltpu.get_barrier_semaphore()

    def y_peer(k):
        return (s, lax.rem(y + k, NY) * NZ + zh)

    z_peer = (s, y * NZ + (1 - zh))
    for to in (y_peer(1), y_peer(2), y_peer(3), z_peer):
        pl.semaphore_signal(barrier, inc=1, device_id=to, device_id_type=MESH)

    @pl.when(has_up)
    def _():
        pl.semaphore_signal(barrier, inc=1, device_id=(s + 1, t), device_id_type=MESH)

    @pl.when(has_down)
    def _():
        pl.semaphore_signal(barrier, inc=1, device_id=(s - 1, t), device_id_type=MESH)

    def widen(w):
        at = pl.ds(pl.multiple_of(w * BS, BS), BS)
        for f in range(frames):
            k = key_raw[f, :, at]
            kf = k.astype(jnp.float32)
            key_cat[w, 0:ck, f * BS : (f + 1) * BS] = (kf * kf).astype(jnp.bfloat16)
            key_cat[w, ck : 2 * ck, f * BS : (f + 1) * BS] = k

    own[0].wait()

    @pl.loop(0, n_blocks)
    def _(b):
        widen(W + b)

    pl.semaphore_wait(barrier, NY + has_up.astype(jnp.int32) + has_down.astype(jnp.int32))

    def remote(src, dst, send, recv, to):
        return pltpu.make_async_remote_copy(
            src_ref=src, dst_ref=dst, send_sem=send, recv_sem=recv, device_id=to, device_id_type=MESH
        )

    top_blocks, low_blocks = pl.ds(n_blocks - W, W), pl.ds(0, W)
    ups, downs = [], []
    for halo, (blocks, dst_at, to) in (
        (ups, (top_blocks, pl.ds(0, W), (s + 1, t))),
        (downs, (low_blocks, pl.ds(W + n_blocks, W), (s - 1, t))),
    ):
        d = 0 if halo is ups else 1
        own_at = pl.ds(n_blocks, W) if halo is ups else pl.ds(W, W)
        key_from = pl.ds(n_own - n_halo, n_halo) if halo is ups else pl.ds(0, n_halo)
        key_to = pl.ds(0, n_halo) if halo is ups else pl.ds(n_halo + n_own, n_halo)
        halo.append(
            remote(
                key_hbm.at[:, :, key_from], key_raw.at[:, :, key_to], halo_send.at[d, 0], halo_recv.at[d, 0], to
            )
        )
        halo.append(remote(shrink_win.at[own_at], shrink_win.at[dst_at], halo_send.at[d, 1], halo_recv.at[d, 1], to))
        for h in range(HALVES):
            halo.append(
                remote(
                    value_hbm.at[:, blocks, :, pl.ds(h * cols, cols)],
                    values[h].at[:, dst_at],
                    halo_send.at[d, 2 + h],
                    halo_recv.at[d, 2 + h],
                    to,
                )
            )

    @pl.when(has_up)
    def _():
        for copy in ups:
            copy.start()

    @pl.when(has_down)
    def _():
        for copy in downs:
            copy.start()

    def halo_arrived(n):
        @pl.when(has_down)
        def _():
            ups[n].wait_recv()

        @pl.when(has_up)
        def _():
            downs[n].wait_recv()

    for copy in own[1:]:
        copy.start()
    for copy in queries:
        copy.wait()

    @pl.loop(0, n_blocks)
    def _(b):
        at = pl.ds(pl.multiple_of(b * BS, BS), BS)
        sel = select_ref[0, :, at].astype(jnp.float32)
        q = query_ref[0, :, at].astype(jnp.float32)
        lhs = jnp.concatenate([sel, -2.0 * q * sel], axis=0).T.astype(jnp.bfloat16)
        self_term = jnp.broadcast_to(jnp.sum(sel * q * q, axis=0, keepdims=True), (BS, BS)).T
        lhs_all[b] = lhs
        self_all[b] = self_term

    halo_arrived(0)
    halo_arrived(1)
    for w in (0, 1, W + n_blocks, W + n_blocks + 1):
        widen(w)

    @pl.loop(0, n_blocks)
    def _(b):
        self_term = jnp.concatenate([self_all[b]] * frames, axis=1)
        live = jnp.full((1, BS), count_ref[b], jnp.int32)
        best = jnp.full((BS, BS), NEG, jnp.float32)
        for j in range(n_listed):
            w = list_ref[b, j]
            dots = jnp.dot(lhs_all[b], key_cat[w], preferred_element_type=jnp.float32)
            score = (dots + self_term) * shrink_win[w]
            scores[j] = score
            most = score[:, 0:BS]
            for f in range(1, frames):
                most = jnp.maximum(most, score[:, f * BS : (f + 1) * BS])
            best = jnp.maximum(best, jnp.where(live > j, most, NEG))
        top = jnp.max(best, axis=1, keepdims=True)
        total = jnp.zeros((BS, BS), jnp.float32)
        for j in range(n_listed):
            under = jnp.where(live > j, jnp.broadcast_to(top, (BS, BS)), -NEG)
            for f in range(frames):
                p = jnp.exp2(scores[j, :, f * BS : (f + 1) * BS] - under)
                weights[b, :, (j * frames + f) * BS : (j * frames + f + 1) * BS] = p.astype(jnp.bfloat16)
                total = total + p
        whole = jnp.sum(total, axis=1, keepdims=True)
        inverse[b] = jnp.broadcast_to(1.0 / whole, (BS, BS))
        lse_y[0, b] = jnp.broadcast_to(top + jnp.log2(whole), (BS, BS)).T[0:1, :]

    def ly_copy(k):
        return remote(lse_y.at[0], lse_y.at[k], ly_send.at[k - 1], ly_recv.at[k - 1], y_peer(k))

    lz_copy = remote(lse_z.at[0], lse_z.at[1], lz_send.at[0], lz_recv.at[0], z_peer)
    for k in range(1, NY):
        ly_copy(k).start()

    def spread(levels, share):
        peak = functools.reduce(jnp.maximum, levels)
        whole = peak + jnp.log2(functools.reduce(jnp.add, [jnp.exp2(level - peak) for level in levels]))
        factors = jnp.concatenate([jnp.exp2(level - whole) for level in levels], axis=0)
        rest = jnp.zeros((BS - factors.shape[0], BS), jnp.float32)
        turned[...] = jnp.concatenate([factors, rest], axis=0).T
        mine = turned[pl.ds(pl.multiple_of(y * rows_y, rows_y), rows_y), :]
        for g in range(len(levels)):
            for b in range(n_blocks):
                n = g * n_blocks + b
                share[g, b] = jnp.broadcast_to(mine[:, n : n + 1], (rows_y, BS))
        return whole

    def level(ref, g):
        return jnp.concatenate([ref[g, b] for b in range(n_blocks)], axis=0)

    def wide(x):
        return jnp.concatenate([x] * (cols // BS), axis=1)

    def y_copy(k, i):
        return remote(part.at[i, lax.rem(y + k, NY)], part_in.at[k - 1, i], y_send.at[k - 1, i], y_recv.at[k - 1, i], y_peer(k))

    def z_copy(i):
        return remote(zsum.at[i], zin.at[i], z_send.at[i], z_recv.at[i], z_peer)

    def out_at(i, yy):
        at = pl.ds(pl.multiple_of(lax.div(i, n_blocks) * cols, cols), cols)
        return out_ref.at[lax.rem(i, n_blocks), yy, :, at]

    def g_copy(k, i):
        return remote(out_at(i, y), out_at(i, y), g_send.at[k - 1, i], g_recv.at[k - 1, i], y_peer(k))

    def g_arrival(k, i):
        at = out_at(i, lax.rem(y + NY - k, NY))
        return remote(out_at(i, y), at, g_send.at[k - 1, i], g_recv.at[k - 1, i], y_peer(k))

    def stage_value(h, b):
        i = h * n_blocks + b
        acc = jnp.zeros((BS, cols), jnp.float32)
        for j in range(n_listed):
            w = list_ref[b, j]
            rhs = jnp.concatenate([values[h][f, w] for f in range(frames)], axis=0)
            acc = acc + jnp.dot(
                weights[b, :, j * group : (j + 1) * group], rhs, preferred_element_type=jnp.float32
            )
        part[i] = (acc * wide(inverse[b])).astype(jnp.bfloat16).reshape(NY, BS // NY, cols)
        for k in range(1, NY):
            y_copy(k, i).start()

    def stage_y(i):
        b = lax.rem(i, n_blocks)
        total = part[i, y].astype(jnp.float32) * wide(share_y[0, b])
        for k in range(1, NY):
            y_copy(k, i).wait_recv()
            total = total + part_in[k - 1, i].astype(jnp.float32) * wide(share_y[k, b])
        zsum[i] = total.astype(jnp.bfloat16)
        z_copy(i).start()

    def stage_z(i):
        b = lax.rem(i, n_blocks)
        z_copy(i).wait_recv()
        mine, other = zsum[i].astype(jnp.float32), zin[i].astype(jnp.float32)
        low, high = jnp.where(zh == 0, mine, other), jnp.where(zh == 0, other, mine)
        out_at(i, y)[...] = (low * wide(share_z[0, b]) + high * wide(share_z[1, b])).astype(jnp.bfloat16)
        for k in range(1, NY):
            g_copy(k, i).start()

    own[1].wait()
    halo_arrived(2)

    @pl.loop(0, LAG_Y)
    def _(b):
        stage_value(0, b)

    for k in range(1, NY):
        ly_copy(k).wait_recv()
    local = spread([level(lse_y, k) for k in range(NY)], share_y)
    for b in range(n_blocks):
        lse_z[0, b] = local[b : b + 1]

    lz_copy.start()

    @pl.loop(LAG_Y, n_blocks)
    def _(b):
        stage_value(0, b)
        stage_y(b - LAG_Y)

    own[2].wait()
    halo_arrived(3)

    @pl.loop(0, LAG_Z)
    def _(b):
        stage_value(1, b)
        stage_y(n_blocks + b - LAG_Y)

    lz_copy.wait_recv()
    mine, other = level(lse_z, 0), level(lse_z, 1)
    spread([jnp.where(zh == 0, mine, other), jnp.where(zh == 0, other, mine)], share_z)

    @pl.loop(LAG_Z, n_blocks)
    def _(b):
        stage_value(1, b)
        stage_y(n_blocks + b - LAG_Y)
        stage_z(b - LAG_Z)

    @pl.loop(pieces - LAG_Y, pieces)
    def _(i):
        stage_y(i)
        stage_z(i + LAG_Y - n_blocks - LAG_Z)

    @pl.loop(n_blocks + LAG_Y - LAG_Z, pieces)
    def _(i):
        stage_z(i)

    @pl.loop(0, pieces)
    def _(i):
        for k in range(1, NY):
            g_arrival(k, i).wait_recv()
            y_copy(k, i).wait_send()
            g_copy(k, i).wait_send()
        z_copy(i).wait_send()

    for k in range(1, NY):
        ly_copy(k).wait_send()
    lz_copy.wait_send()

    @pl.when(has_up)
    def _():
        for copy in ups:
            copy.wait_send()

    @pl.when(has_down)
    def _():
        for copy in downs:
            copy.wait_send()


def hand_over(x_ref, out_ref, held, in_sem, out_sem):
    rows = x_ref.shape[1] // N_COPIES
    ins, outs = [], []
    for n in range(N_COPIES):
        at = pl.ds(n * rows, rows)
        ins.append(pltpu.make_async_copy(x_ref.at[:, at], held.at[:, at], in_sem.at[n]))
        outs.append(pltpu.make_async_copy(held.at[:, at], out_ref.at[:, at], out_sem.at[n]))
    for copy in ins:
        copy.start()
    for n in range(N_COPIES):
        ins[n].wait()
        outs[n].start()
    for copy in outs:
        copy.wait()


def shards(n_space, query_key, selection, memory_key, shrinkage, memory_value, block_list, block_count):
    frames, pixels, ck = memory_key.shape
    query_key, selection = query_key.transpose(0, 2, 1), selection.transpose(0, 2, 1)
    cv = memory_value.shape[2]
    n_blocks = pixels // BS
    n_listed = block_list.shape[1]
    window = n_blocks + 2 * W
    cols = cv // HALVES
    pieces = HALVES * n_blocks
    part_rows = BS // NY
    bf, f32 = jnp.bfloat16, jnp.float32
    keys = memory_key.transpose(0, 2, 1)
    vals = memory_value.reshape(frames, n_blocks, BS, cv)
    vmem = pl.BlockSpec(memory_space=pltpu.VMEM)
    smem = pl.BlockSpec(memory_space=pltpu.SMEM)
    hbm = pl.BlockSpec(memory_space=pltpu.HBM)
    dma = pltpu.SemaphoreType.DMA
    out = pl.pallas_call(
        functools.partial(kernel, n_space),
        out_shape=jax.ShapeDtypeStruct((n_blocks, NY, part_rows, cv), bf),
        in_specs=[smem, smem, hbm, hbm, vmem, hbm, hbm],
        out_specs=vmem,
        scratch_shapes=[
            pltpu.VMEM((1, ck, pixels), bf),
            pltpu.VMEM((1, ck, pixels), bf),
            pltpu.VMEM((n_blocks, BS, 2 * ck), bf),
            pltpu.VMEM((n_blocks, BS, BS), f32),
            pltpu.VMEM((frames, ck, window * BS), bf),
            pltpu.VMEM((window, 2 * ck, frames * BS), bf),
            pltpu.VMEM((window, 1, frames * BS), f32),
            pltpu.VMEM((frames, window, BS, cols), bf),
            pltpu.VMEM((frames, window, BS, cols), bf),
            pltpu.VMEM((n_blocks, BS, n_listed * frames * BS), bf),
            pltpu.VMEM((n_listed, BS, frames * BS), f32),
            pltpu.VMEM((n_blocks, BS, BS), f32),
            pltpu.VMEM((NY, n_blocks, 1, BS), f32),
            pltpu.VMEM((NZ, n_blocks, 1, BS), f32),
            pltpu.VMEM((BS, BS), f32),
            pltpu.VMEM((NY, n_blocks, part_rows, BS), f32),
            pltpu.VMEM((NZ, n_blocks, part_rows, BS), f32),
            pltpu.VMEM((pieces, NY, part_rows, cols), bf),
            pltpu.VMEM((NY - 1, pieces, part_rows, cols), bf),
            pltpu.VMEM((pieces, part_rows, cols), bf),
            pltpu.VMEM((pieces, part_rows, cols), bf),
            dma((3 + HALVES,)),
            dma((2, 2 + HALVES)),
            dma((2, 2 + HALVES)),
            dma((NY - 1,)),
            dma((NY - 1,)),
            dma((1,)),
            dma((1,)),
            dma((NY - 1, pieces)),
            dma((NY - 1, pieces)),
            dma((pieces,)),
            dma((pieces,)),
            dma((NY - 1, pieces)),
            dma((NY - 1, pieces)),
        ],
        compiler_params=pltpu.CompilerParams(
            collective_id=0, has_side_effects=True, vmem_limit_bytes=60 << 20
        ),
    )(block_list, block_count, query_key, selection, shrinkage, keys, vals)
    return pl.pallas_call(
        hand_over,
        out_shape=jax.ShapeDtypeStruct((1, pixels, cv), bf),
        in_specs=[hbm],
        out_specs=hbm,
        scratch_shapes=[pltpu.VMEM((1, pixels, cv), bf), dma((N_COPIES,)), dma((N_COPIES,))],
    )(out.reshape(1, pixels, cv))


def solution(mesh):
    in_specs = (
        P(None, "space", None),
        P(None, "space", None),
        P("tm", "space", None),
        P("tm", "space"),
        P("tm", "space", None),
        P("space", None),
        P("space"),
    )
    out_specs = P(None, "space", None)
    return jax.shard_map(
        functools.partial(shards, mesh.shape["space"]),
        mesh=mesh,
        in_specs=in_specs,
        out_specs=out_specs,
        check_vma=False,
    )
```

time: 97.8 us -> 66.4 us (0.68)
  the two profiles are of different devices: /device:TPU:32 before, /device:TPU:39 now
where the time goes in v2:
time: 66.4 us; the launch traced here: 66.2 us
  Pallas kernels  66.2 us (100%)
    pallas_call x1, Pallas kernels, shards(): pl.pallas_call(functools.partial(kernel, n_space), out_shape=jax.ShapeDty...  64.2 us
    pallas_call x1, Pallas kernels, shards(): pl.pallas_call(hand_over, out_shape=jax.ShapeDtypeStruct((1, pixels, cv),...  1.98 us

profile of v2, /device:TPU:39, one launch (start us, length us, event | category | flops | bytes accessed | tf_op | source)
XLA Modules:
  0.0 66.2 jit_solution(9044463578947361744)
XLA Ops:
  0.0 64.2 %shard_map.73 = bf16[8,4,32,512]{3,2,1,0:T(8,128)(2,1)} custom-call(s32[8,6]{1,0:T(8,128)} %list_ref.1, s32[8]{0:T(128)} %count_ref.1, bf16[1,64,1024]{2,1,0:T(8,128)(2,1)} %bitcast.8, bf16[1,64,1024]{2,1,0:T(8,128)(2,1)} %bitcast.9, bf16[4,1024]{1,0:T(4,128)(2,1)} %shrink_ref.1, bf16[4,64,1024]{2,1,0:T(8,128)(2,1)} %bitcast.7, bf16[4,8,128,512]{3,2,1,0:T(8,128)(2,1)} %bitcast.5), custom_call_target="tpu_custom_call" | custom-call | tf_op jit(solution)/shard_map/pallas_call | solution.py:388
  64.2 2.0 %shard_map.74 = bf16[1,1024,512]{2,1,0:T(8,128)(2,1)} custom-call(bf16[1,1024,512]{2,1,0:T(8,128)(2,1)} %bitcast.6), custom_call_target="tpu_custom_call" | custom-call | tf_op jit(solution)/shard_map/pallas_call | solution.py:433

commit v3 on v2

--- a/solution.py
+++ b/solution.py
@@ -13,9 +13,9 @@
 NY = 4
 NZ = 2
 HALVES = 2
-LAG_Y = 6
-LAG_Z = 7
+LAG_Y = 3
 N_COPIES = 4
+FAR_FIRST = (2, 1, 3)
 NEG = -1e30
 MESH = pl.DeviceIdType.MESH
 
@@ -143,15 +143,17 @@
                 )
             )
 
-    @pl.when(has_up)
-    def _():
-        for copy in ups:
-            copy.start()
-
-    @pl.when(has_down)
-    def _():
-        for copy in downs:
-            copy.start()
+    for first, last in ((0, 2), (2, 3), (3, 4)):
+
+        @pl.when(has_up)
+        def _():
+            for copy in ups[first:last]:
+                copy.start()
+
+        @pl.when(has_down)
+        def _():
+            for copy in downs[first:last]:
+                copy.start()
 
     def halo_arrived(n):
         @pl.when(has_down)
@@ -261,7 +263,7 @@
                 weights[b, :, j * group : (j + 1) * group], rhs, preferred_element_type=jnp.float32
             )
         part[i] = (acc * wide(inverse[b])).astype(jnp.bfloat16).reshape(NY, BS // NY, cols)
-        for k in range(1, NY):
+        for k in FAR_FIRST:
             y_copy(k, i).start()
 
     def stage_y(i):
@@ -279,7 +281,7 @@
         mine, other = zsum[i].astype(jnp.float32), zin[i].astype(jnp.float32)
         low, high = jnp.where(zh == 0, mine, other), jnp.where(zh == 0, other, mine)
         out_at(i, y)[...] = (low * wide(share_z[0, b]) + high * wide(share_z[1, b])).astype(jnp.bfloat16)
-        for k in range(1, NY):
+        for k in FAR_FIRST:
             g_copy(k, i).start()
 
     own[1].wait()
@@ -305,7 +307,7 @@
     own[2].wait()
     halo_arrived(3)
 
-    @pl.loop(0, LAG_Z)
+    @pl.loop(0, n_blocks)
     def _(b):
         stage_value(1, b)
         stage_y(n_blocks + b - LAG_Y)
@@ -314,18 +316,12 @@
     mine, other = level(lse_z, 0), level(lse_z, 1)
     spread([jnp.where(zh == 0, mine, other), jnp.where(zh == 0, other, mine)], share_z)
 
-    @pl.loop(LAG_Z, n_blocks)
-    def _(b):
-        stage_value(1, b)
-        stage_y(n_blocks + b - LAG_Y)
-        stage_z(b - LAG_Z)
-
     @pl.loop(pieces - LAG_Y, pieces)
     def _(i):
         stage_y(i)
-        stage_z(i + LAG_Y - n_blocks - LAG_Z)
-
-    @pl.loop(n_blocks + LAG_Y - LAG_Z, pieces)
+        stage_z(i + LAG_Y - pieces)
+
+    @pl.loop(LAG_Y, pieces)
     def _(i):
         stage_z(i)
 

time: 66.4 us -> 65.2 us (0.982)
  Pallas kernels: 66.2 us -> 64.8 us
    pallas_call x1, Pallas kernels: 64.2 us -> 62.8 us  [shards(): pl.pallas_call(functools.partial(kernel, n_space), out_shape=jax.ShapeDty...]
where the time goes in v3:
time: 65.2 us; the launch traced here: 64.8 us
  Pallas kernels  64.8 us (99%)
    pallas_call x1, Pallas kernels, shards(): pl.pallas_call(functools.partial(kernel, n_space), out_shape=jax.ShapeDty...  62.8 us
    pallas_call x1, Pallas kernels, shards(): pl.pallas_call(hand_over, out_shape=jax.ShapeDtypeStruct((1, pixels, cv),...  1.98 us

profile of v3, /device:TPU:39, one launch (start us, length us, event | category | flops | bytes accessed | tf_op | source)
XLA Modules:
  0.0 64.8 jit_solution(12752568079005762238)
XLA Ops:
  0.0 62.8 %shard_map.73 = bf16[8,4,32,512]{3,2,1,0:T(8,128)(2,1)} custom-call(s32[8,6]{1,0:T(8,128)} %list_ref.1, s32[8]{0:T(128)} %count_ref.1, bf16[1,64,1024]{2,1,0:T(8,128)(2,1)} %bitcast.8, bf16[1,64,1024]{2,1,0:T(8,128)(2,1)} %bitcast.9, bf16[4,1024]{1,0:T(4,128)(2,1)} %shrink_ref.1, bf16[4,64,1024]{2,1,0:T(8,128)(2,1)} %bitcast.7, bf16[4,8,128,512]{3,2,1,0:T(8,128)(2,1)} %bitcast.5), custom_call_target="tpu_custom_call" | custom-call | tf_op jit(solution)/shard_map/pallas_call | solution.py:384
  62.8 2.0 %shard_map.74 = bf16[1,1024,512]{2,1,0:T(8,128)(2,1)} custom-call(bf16[1,1024,512]{2,1,0:T(8,128)(2,1)} %bitcast.6), custom_call_target="tpu_custom_call" | custom-call | tf_op jit(solution)/shard_map/pallas_call | solution.py:429
